TPU v7x, 32 devices: a whole 2x2x4 slice. The times are simulated.
32 devices in a mesh: win: 4 (over z), seq: 8 (over y, x, core).
Axes of the slice: x: 2, y: 2, z: 4, core: 2. Of those that a mesh axis runs over, the one named last changes fastest.
Arguments:
- layer_input: bfloat16 [8, 1024, 768], P('win', 'seq'), may hold values from -6 to 6
- d_out: bfloat16 [8, 1024, 768], P('win', 'seq'), may hold values from -13.5 to 13.5
- rand_ids: int32 [8, 16, 12, 3], P('win', 'seq'), may hold values from 0 to 15
- live_mask: int32 [8], P('win'), may hold values 0 or 1
- w_qkv: float32 [768, 2304], P('seq', 'win'), may hold values from -0.21875 to 0.21875
- w_out: float32 [768, 768], P('seq', 'win'), may hold values from -0.875 to 0.875
- w_up: float32 [768, 3072], P('seq', 'win'), may hold values from -0.25259074 to 0.25259074
- w_down: float32 [3072, 768], P('seq', 'win'), may hold values from -0.109375 to 0.109375
- norm_params: float32 [3072], P(('win', 'seq')), may hold values from -1.2 to 2, as said below
- m_qkv: float32 [768, 2304], P('seq', 'win'), may hold values from -0.0015031901 to 0.0015031901, as said below
- m_out: float32 [768, 768], P('seq', 'win'), may hold values from -0.0015031901 to 0.0015031901, as said below
- m_up: float32 [768, 3072], P('seq', 'win'), may hold values from -0.0015031901 to 0.0015031901, as said below
- m_down: float32 [3072, 768], P('seq', 'win'), may hold values from -0.0015031901 to 0.0015031901, as said below
- m_norm: float32 [3072], P(('win', 'seq')), may hold values from -0.0060127606 to 0.0060127606, as said below
- v_qkv: float32 [768, 2304], P('seq', 'win'), may hold values from 1.412238e-07 to 5.648952e-07
- v_out: float32 [768, 768], P('seq', 'win'), may hold values from 1.412238e-07 to 5.648952e-07
- v_up: float32 [768, 3072], P('seq', 'win'), may hold values from 1.412238e-07 to 5.648952e-07
- v_down: float32 [3072, 768], P('seq', 'win'), may hold values from 1.412238e-07 to 5.648952e-07
- v_norm: float32 [3072], P(('win', 'seq')), may hold values from 2.2595806e-06 to 9.0383225e-06
Outputs:
- output: bfloat16 [8, 1024, 768], P('win', 'seq')
- d_input: float32 [8, 1024, 768], P('win', 'seq')
- g_qkv: float32 [768, 2304], P('seq', 'win')
- g_out: float32 [768, 768], P('seq', 'win')
- g_up: float32 [768, 3072], P('seq', 'win')
- g_down: float32 [3072, 768], P('seq', 'win')
- g_norm: float32 [3072], P(('win', 'seq'))
- new_qkv: float32 [768, 2304], P('seq', 'win')
- new_out: float32 [768, 768], P('seq', 'win')
- new_up: float32 [768, 3072], P('seq', 'win')
- new_down: float32 [3072, 768], P('seq', 'win')
- new_norm: float32 [3072], P(('win', 'seq'))
- mom_qkv: float32 [768, 2304], P('seq', 'win')
- mom_out: float32 [768, 768], P('seq', 'win')
- mom_up: float32 [768, 3072], P('seq', 'win')
- mom_down: float32 [3072, 768], P('seq', 'win')
- mom_norm: float32 [3072], P(('win', 'seq'))
- sec_qkv: float32 [768, 2304], P('seq', 'win')
- sec_out: float32 [768, 768], P('seq', 'win')
- sec_up: float32 [768, 3072], P('seq', 'win')
- sec_down: float32 [3072, 768], P('seq', 'win')
- sec_norm: float32 [3072], P(('win', 'seq'))
- grad_norm: float32 [1], replicated
Inputs may be any that keep to these rules, and one draw needn't show every extreme that they name: `norm_params`: gains about 1 in the first and third pieces, shifts of both signs in the second and fourth. `m_qkv`: of both signs. `m_out`: of both signs. `m_up`: of both signs. `m_down`: of both signs. `m_norm`: of both signs.
All inputs are finite; a program needn't handle non-finite values. No bound on the sum of `live_mask` on one device may be relied on, other than what follows from the above.
Results may differ from a plain program's by a relative error of at most 0.035.
Values may be sent and summed in bfloat16 or wider, within the bound.
A program may use at most 320 MiB of HBM per device.

v0:
```python
import math
import jax
import jax.numpy as jnp
from jax import lax
from jax.sharding import PartitionSpec as P

H = 12
HD = 64
BLK = 64
STEP = 3
NEG = -1e30
ln_eps = 1e-05
beta_one = 0.5
beta_two = 0.5
adam_eps = 1e-08
decay_rate = 0.1
rate_matrix = 0.04
rate_output = 0.16
rate_norm = 0.6


def layer_norm(values, gain, shift):
    centre = values - jnp.mean(values, axis=-1, keepdims=True)
    spread = jnp.mean(centre * centre, axis=-1, keepdims=True)
    return centre * lax.rsqrt(spread + ln_eps) * gain + shift


def slot_counts(rand_ids, first_block, block_count):
    blocks_dev = rand_ids.shape[1]
    here = (first_block + jnp.arange(blocks_dev, dtype=jnp.int32))[:, None]
    every = jnp.arange(block_count, dtype=jnp.int32)[None, :]
    near = (jnp.abs(here - every) <= 1).astype(jnp.float32)
    ends = (every == 0).astype(jnp.float32) + (every == block_count - 1).astype(jnp.float32)
    drawn = jnp.sum((rand_ids[..., None] == every[0]).astype(jnp.float32), axis=3)
    return (near + ends)[None, :, None, :] + drawn


def adam_update(weight, grad, first, second, rate, decay, fix_one, fix_two):
    first_new = beta_one * first + (1.0 - beta_one) * grad
    second_new = beta_two * second + (1.0 - beta_two) * grad * grad
    stride = first_new / fix_one / (jnp.sqrt(second_new / fix_two) + adam_eps)
    return (weight - rate * (stride + decay * weight), first_new, second_new)


def per_device(
    layer_input,
    d_out,
    rand_ids,
    live_mask,
    w_qkv,
    w_out,
    w_up,
    w_down,
    norm_params,
    m_qkv,
    m_out,
    m_up,
    m_down,
    m_norm,
    v_qkv,
    v_out,
    v_up,
    v_down,
    v_norm,
):
    wins, local_len, width = layer_input.shape
    blocks_dev = local_len // BLK
    block_count = blocks_dev * lax.axis_size("seq")
    first_block = lax.axis_index("seq") * blocks_dev
    inv_root = 1.0 / math.sqrt(HD)
    rows = wins * local_len
    low_qkv = w_qkv.astype(jnp.bfloat16)
    low_out = w_out.astype(jnp.bfloat16)
    low_up = w_up.astype(jnp.bfloat16)
    low_down = w_down.astype(jnp.bfloat16)
    low_norm = norm_params.astype(jnp.bfloat16)
    full_qkv, full_out, full_up, full_down = (
        lax.all_gather(lax.all_gather(low, "win", axis=1, tiled=True), "seq", axis=0, tiled=True)
        for low in (low_qkv, low_out, low_up, low_down)
    )
    full_norm = lax.all_gather(low_norm, ("win", "seq"), axis=0, tiled=True)
    gains = full_norm.astype(jnp.float32).reshape(4, width)
    loss_weight = live_mask.astype(jnp.float32)
    counts = slot_counts(rand_ids, first_block, block_count)
    bias = jnp.where(counts > 0, jnp.log(jnp.maximum(counts, 1.0)), NEG)
    bias = jnp.repeat(bias, BLK, axis=3)[:, :, :, None, :]
    tokens = layer_input.astype(jnp.float32).reshape(rows, width)
    h_one = layer_norm(tokens, gains[0], gains[1]).astype(jnp.bfloat16)
    qkv = jnp.dot(h_one, full_qkv, preferred_element_type=jnp.float32)
    q_heads = qkv[:, :width].astype(jnp.bfloat16).reshape(wins, blocks_dev, BLK, H, HD)
    keyval = qkv[:, width:].astype(jnp.bfloat16).reshape(wins, local_len, 2 * width)
    window = lax.all_gather(keyval, "seq", axis=1, tiled=True)
    shaped = window.reshape(wins, block_count * BLK, 2, H, HD)
    keys, values = (shaped[:, :, 0], shaped[:, :, 1])
    scores = (
        jnp.einsum("wbqhd,wkhd->wbhqk", q_heads, keys, preferred_element_type=jnp.float32)
        * inv_root
        + bias
    )
    top = jnp.max(scores, axis=-1, keepdims=True)
    log_total = top + jnp.log(jnp.sum(jnp.exp(scores - top), axis=-1, keepdims=True))
    prob = jnp.exp(scores - log_total).astype(jnp.bfloat16)
    heads_out = jnp.einsum("wbhqk,wkhd->wbqhd", prob, values, preferred_element_type=jnp.float32)
    attended = heads_out.astype(jnp.bfloat16).reshape(rows, width)
    middle = tokens + jnp.dot(attended, full_out, preferred_element_type=jnp.float32)
    h_two = layer_norm(middle, gains[2], gains[3]).astype(jnp.bfloat16)
    up_proj = jnp.dot(h_two, full_up, preferred_element_type=jnp.float32)
    active = jax.nn.gelu(up_proj).astype(jnp.bfloat16)
    result = middle + jnp.dot(active, full_down, preferred_element_type=jnp.float32)
    output = result.astype(jnp.bfloat16).reshape(wins, local_len, width)
    grad_y = (d_out.astype(jnp.float32) * loss_weight[:, None, None]).reshape(rows, width)
    grad_ffn = grad_y.astype(jnp.bfloat16)
    raw_down = jnp.einsum("tf,td->fd", active, grad_ffn, preferred_element_type=jnp.float32)
    grad_act = jnp.einsum("td,fd->tf", grad_ffn, full_down, preferred_element_type=jnp.float32)
    gelu_pull = jax.vjp(jax.nn.gelu, up_proj)[1]
    grad_up = gelu_pull(grad_act)[0].astype(jnp.bfloat16)
    raw_up = jnp.einsum("td,tf->df", h_two, grad_up, preferred_element_type=jnp.float32)
    grad_h_two = jnp.einsum("tf,df->td", grad_up, full_up, preferred_element_type=jnp.float32)
    norm_pull = jax.vjp(layer_norm, middle, gains[2], gains[3])[1]
    grad_mid_ln, raw_gain_two, raw_shift_two = norm_pull(grad_h_two)
    grad_mid = grad_y + grad_mid_ln
    grad_att = grad_mid.astype(jnp.bfloat16)
    raw_out = jnp.einsum("td,te->de", attended, grad_att, preferred_element_type=jnp.float32)
    grad_o = jnp.einsum("te,de->td", grad_att, full_out, preferred_element_type=jnp.float32)
    grad_o = grad_o.astype(jnp.bfloat16).reshape(wins, blocks_dev, BLK, H, HD)
    grad_p = jnp.einsum("wbqhd,wkhd->wbhqk", grad_o, values, preferred_element_type=jnp.float32)
    prob_f = prob.astype(jnp.float32)
    inner = jnp.sum(prob_f * grad_p, axis=-1, keepdims=True)
    grad_s = (prob_f * (grad_p - inner)).astype(jnp.bfloat16)
    grad_q = (
        jnp.einsum("wbhqk,wkhd->wbqhd", grad_s, keys, preferred_element_type=jnp.float32) * inv_root
    )
    grad_v = jnp.einsum("wbhqk,wbqhd->wkhd", prob, grad_o, preferred_element_type=jnp.float32)
    grad_k = (
        jnp.einsum("wbhqk,wbqhd->wkhd", grad_s, q_heads, preferred_element_type=jnp.float32)
        * inv_root
    )
    grad_kv = jnp.stack([grad_k, grad_v], axis=2).astype(jnp.bfloat16)
    grad_kv = lax.psum_scatter(
        grad_kv.reshape(wins, block_count * BLK, 2 * width), "seq", scatter_dimension=1, tiled=True
    ).reshape(rows, 2 * width)
    grad_qkv = jnp.concatenate([grad_q.reshape(rows, width).astype(jnp.bfloat16), grad_kv], axis=1)
    raw_qkv = jnp.einsum("td,te->de", h_one, grad_qkv, preferred_element_type=jnp.float32)
    grad_h_one = jnp.einsum("te,de->td", grad_qkv, full_qkv, preferred_element_type=jnp.float32)
    first_pull = jax.vjp(layer_norm, tokens, gains[0], gains[1])[1]
    grad_tok_ln, raw_gain_one, raw_shift_one = first_pull(grad_h_one)
    d_input = (grad_mid + grad_tok_ln).reshape(wins, local_len, width)
    raw_norm = jnp.concatenate([raw_gain_one, raw_shift_one, raw_gain_two, raw_shift_two])
    red_qkv, red_out, red_up, red_down = (
        lax.psum_scatter(
            lax.psum_scatter(raw.astype(jnp.bfloat16), "seq", scatter_dimension=0, tiled=True),
            "win",
            scatter_dimension=1,
            tiled=True,
        ).astype(jnp.float32)
        for raw in (raw_qkv, raw_out, raw_up, raw_down)
    )
    red_norm = lax.psum_scatter(raw_norm, ("win", "seq"), scatter_dimension=0, tiled=True)
    reduced = (red_qkv, red_out, red_up, red_down, red_norm)
    local_squares = jnp.float32(0.0)
    for grad in reduced:
        local_squares = local_squares + jnp.sum(grad * grad)
    grad_norm = jnp.sqrt(lax.psum(local_squares, ("win", "seq")))
    factor = 1.0 / jnp.maximum(grad_norm, 1.0)
    clipped = tuple((grad * factor for grad in reduced))
    count = jnp.float32(STEP)
    fix_one = 1.0 - jnp.power(jnp.float32(beta_one), count)
    fix_two = 1.0 - jnp.power(jnp.float32(beta_two), count)
    params = (w_qkv, w_out, w_up, w_down, norm_params)
    firsts = (m_qkv, m_out, m_up, m_down, m_norm)
    seconds = (v_qkv, v_out, v_up, v_down, v_norm)
    rates = (rate_matrix, rate_output, rate_matrix, rate_matrix, rate_norm)
    news, moms, secs = ([], [], [])
    for index in range(5):
        decay = 0.0 if index == 4 else decay_rate
        new_w, new_m, new_v = adam_update(
            params[index],
            clipped[index],
            firsts[index],
            seconds[index],
            rates[index],
            decay,
            fix_one,
            fix_two,
        )
        news.append(new_w)
        moms.append(new_m)
        secs.append(new_v)
    return (
        output,
        d_input,
        clipped[0],
        clipped[1],
        clipped[2],
        clipped[3],
        clipped[4],
        news[0],
        news[1],
        news[2],
        news[3],
        news[4],
        moms[0],
        moms[1],
        moms[2],
        moms[3],
        moms[4],
        secs[0],
        secs[1],
        secs[2],
        secs[3],
        secs[4],
        grad_norm.reshape(1),
    )


def solution(mesh):
    placed = (
        P("win", "seq", None),
        P("win", "seq", None),
        P("win", "seq", None, None),
        P("win"),
        P("seq", "win"),
        P("seq", "win"),
        P("seq", "win"),
        P("seq", "win"),
        P(("win", "seq")),
        P("seq", "win"),
        P("seq", "win"),
        P("seq", "win"),
        P("seq", "win"),
        P(("win", "seq")),
        P("seq", "win"),
        P("seq", "win"),
        P("seq", "win"),
        P("seq", "win"),
        P(("win", "seq")),
    )
    return jax.shard_map(
        per_device,
        mesh=mesh,
        in_specs=placed,
        out_specs=(
            P("win", "seq", None),
            P("win", "seq", None),
            P("seq", "win"),
            P("seq", "win"),
            P("seq", "win"),
            P("seq", "win"),
            P(("win", "seq")),
            P("seq", "win"),
            P("seq", "win"),
            P("seq", "win"),
            P("seq", "win"),
            P(("win", "seq")),
            P("seq", "win"),
            P("seq", "win"),
            P("seq", "win"),
            P("seq", "win"),
            P(("win", "seq")),
            P("seq", "win"),
            P("seq", "win"),
            P("seq", "win"),
            P("seq", "win"),
            P(("win", "seq")),
            P(),
        ),
        check_vma=False,
    )
```

profile of v0, /device:TPU:0, one launch (start us, length us, event | category | flops | bytes accessed | tf_op | source)
XLA Modules:
  0.0 680.8 jit_solution(3838037226972411840)
XLA Ops:
  8.3 17.0 %all-gather = bf16[4,576,96]{1,2,0:T(8,128)(2,1)S(1)} all-gather(bf16[1,576,96]{1,2,0:T(8,128)(2,1)S(1)} %convert_bitcast_fusion), channel_id=1, replica_groups=mesh['win'=4,'seq'=8] {'win'}, dimensions={0}, use_global_device_ids=true | all-gather | bytes 552960 | tf_op jit(solution)/shard_map/all_gather | solution.py:78
  26.8 17.4 %all_gather.38 = bf16[384,768]{0,1:T(8,128)(2,1)} all-gather(bf16[384,192]{0,1:T(8,128)(2,1)S(1)} %convert_element_type.148), channel_id=1, replica_groups=mesh['win'=4,'seq'=8] {'win'}, dimensions={1}, use_global_device_ids=true | all-gather | bytes 737280 | tf_op jit(solution)/shard_map/all_gather | solution.py:78
  44.6 39.8 %all-reduce = bf16[3072]{0:T(1024)(128)(2,1)S(1)} all-reduce(bf16[3072]{0:T(1024)(128)(2,1)S(1)} %dynamic-update-slice), channel_id=1, replica_groups=mesh['win'=4,'seq'=8] {'win','seq'}, use_global_device_ids=true, to_apply=%add | all-reduce | flops 3072 | bytes 12288
  90.3 14.1 %all_gather.34 = bf16[96,768]{0,1:T(8,128)(2,1)S(1)} all-gather(bf16[96,192]{0,1:T(8,128)(2,1)S(1)} %copy.161), channel_id=1, replica_groups=mesh['win'=4,'seq'=8] {'win'}, dimensions={1}, use_global_device_ids=true | all-gather | bytes 184320 | tf_op jit(solution)/shard_map/all_gather | solution.py:78
  105.3 16.1 %all_gather.36 = bf16[96,3072]{1,0:T(8,128)(2,1)} all-gather(bf16[96,768]{1,0:T(8,128)(2,1)S(1)} %convert_element_type.146), channel_id=1, replica_groups=mesh['win'=4,'seq'=8] {'win'}, dimensions={1}, use_global_device_ids=true | all-gather | bytes 737280 | tf_op jit(solution)/shard_map/all_gather | solution.py:78
  130.6 23.8 %all-gather.9.cloned.1.call-done = bf16[2,1024,1536]{1,2,0:T(8,128)(2,1)} async-done(((bf16[2,128,1536]{1,2,0:T(8,128)(2,1)}), bf16[2,1024,1536]{1,2,0:T(8,128)(2,1)}) %all-gather.9.cloned.1.call-update) | async-done | bytes 6291472 | tf_op jit(solution)/shard_map/all_gather | solution.py:92
  165.0 7.3 %fusion.30 = bf16[2,2,64,12,64]{2,4,1,3,0:T(8,128)(2,1)S(1)} fusion(bf16[2,2,12,64,1024]{4,3,1,2,0:T(8,128)(2,1)S(1)} %exponential_convert_fusion, bf16[2,1024,2,12,64]{1,4,3,2,0:T(8,128)(2,1)} %bitcast.173), kind=kOutput, calls=%fused_computation.43 | convolution fusion | flops 402849792 | bytes 9830400 | tf_op jit(solution)/shard_map/wbhqk,wkhd->wbqhd/dot_general | solution.py:103
  173.6 7.1 %all-gather.11.cloned.1.call-done = bf16[768,768]{1,0:T(8,128)(2,1)} async-done(((bf16[96,768]{1,0:T(8,128)(2,1)}), bf16[768,768]{1,0:T(8,128)(2,1)}) %all-gather.11.cloned.1.call-update) | async-done | bytes 1179664 | tf_op jit(solution)/shard_map/all_gather | solution.py:78
  182.9 38.6 %all-gather.13.cloned.1.call-done = bf16[768,3072]{1,0:T(8,128)(2,1)} async-done(((bf16[96,3072]{1,0:T(8,128)(2,1)}), bf16[768,3072]{1,0:T(8,128)(2,1)}) %all-gather.13.cloned.1.call-update) | async-done | bytes 4718608 | tf_op jit(solution)/shard_map/all_gather | solution.py:78
  221.4 7.8 %fusion.10 = (bf16[256,3072]{1,0:T(8,128)(2,1)S(1)}, f32[256,3072]{1,0:T(8,128)}) fusion(f32[256,3072]{1,0:T(8,128)} %fusion.66, bf16[768,3072]{1,0:T(8,128)(2,1)} %all-gather.13.cloned.1.call-done, f32[256,768]{1,0:T(8,128)S(1)} %get-tuple-element.196, f32[768]{0:T(1024)S(1)} %get-tuple-element.190, f32[768]{0:T(1024)S(1)} %get-tuple-element.189, ...), kind=kOutput, calls=%fused_computation.24 | convolution fusion | flops 1224671232 | bytes 13377536 | tf_op jit(solution)/shard_map/dot_general | solution.py:107
  232.9 6.3 convolution_convert_fusion
  261.9 7.8 %fusion = f32[2,2,12,64]{3,1,2,0:T(2,128)S(1)} fusion(f32[2,2,12,64,1024]{4,3,1,2,0:T(8,128)} %bitcast.165, bf16[2,2,12,64,1024]{4,3,1,2,0:T(8,128)(2,1)} %copy-done.1), kind=kLoop, calls=%fused_computation.2 | loop fusion | flops 9434112 | bytes 18886656 | tf_op jit(solution)/shard_map/reduce_sum | solution.py:128
  269.7 9.6 %fusion.1 = bf16[2,2,12,64,1024]{4,3,1,2,0:T(8,128)(2,1)S(1)} fusion(f32[2,2,12,64]{3,1,2,0:T(2,128)S(1)} %fusion, f32[2,12,1024,128]{2,3,1,0} %fusion.13, f32[2,2,12,64]{3,1,2,0:T(2,128)S(1)} %bitcast.188, f32[2,2,12,1024]{3,1,2,0:T(2,128)S(1)} %copy-done.8, f32[2,12,1024,128]{2,3,1,0} %copy-done), kind=kLoop, calls=%fused_computation.3 | loop fusion | flops 25165824 | bytes 31678464 | tf_op jit(solution)/shard_map/convert_element_type | solution.py:129
  288.3 16.6 %copy.184 = bf16[2,1024,1536]{2,0,1:T(2,128)(2,1)} copy(bf16[2,1024,1536]{1,2,0:T(8,128)(2,1)} %bitcast.167) | data formatting | bytes 12582912
  304.9 7.2 %copy.200 = bf16[128,8,2,1536]{3,1,2,0:T(8,128)(2,1)} copy(bf16[128,8,2,1536]{3,2,1,0:T(2,128)(2,1)} %bitcast.168) | data formatting | bytes 12582912
  313.9 13.7 %reduce-scatter.26.cloned.1.call-done = bf16[384,768]{1,0:T(8,128)(2,1)} async-done(((bf16[3072,768]{1,0:T(8,128)(2,1)}), bf16[384,768]{1,0:T(8,128)(2,1)}) %reduce-scatter.26.cloned.1.call-update) | async-done | bytes 589840 | tf_op jit(solution)/shard_map/reduce_scatter | solution.py:151
  329.8 55.2 %reduce-scatter.22.cloned.1.call-done = bf16[96,3072]{1,0:T(8,128)(2,1)} async-done(((bf16[768,3072]{1,0:T(8,128)(2,1)}), bf16[96,3072]{1,0:T(8,128)(2,1)}) %reduce-scatter.22.cloned.1.call-update) | async-done | bytes 589840 | tf_op jit(solution)/shard_map/reduce_scatter | solution.py:151
  385.2 6.9 %fusion.33 = bf16[2,2,64,12,64]{2,4,1,3,0:T(8,128)(2,1)S(1)} fusion(bf16[2,2,12,64,1024]{4,3,1,2,0:T(8,128)(2,1)} %copy-done.2, bf16[2,1024,2,12,64]{1,4,3,2,0:T(8,128)(2,1)} %bitcast.174), kind=kOutput, calls=%fused_computation.44 | convolution fusion | flops 403046400 | bytes 9830400 | tf_op jit(solution)/shard_map/wbhqk,wkhd->wbqhd/dot_general | solution.py:131
  396.3 54.2 %reduce-scatter.28.cloned.1.call-done = bf16[128,3072]{1,0:T(8,128)(2,1)} async-done(((bf16[1024,3072]{1,0:T(8,128)(2,1)}), bf16[128,3072]{1,0:T(8,128)(2,1)}) %reduce-scatter.28.cloned.1.call-update) | async-done | bytes 786448
  474.1 21.1 %reduce-scatter.34.cloned.1.call-done = bf16[192,384]{1,0:T(8,128)(2,1)} async-done(((bf16[768,384]{1,0:T(8,128)(2,1)}), bf16[192,384]{1,0:T(8,128)(2,1)}) %reduce-scatter.34.cloned.1.call-update) | async-done | bytes 147472
  496.2 21.6 %reduce-scatter.24.cloned.1.call-done = bf16[96,768]{1,0:T(8,128)(2,1)} async-done(((bf16[96,3072]{1,0:T(8,128)(2,1)}), bf16[96,768]{1,0:T(8,128)(2,1)}) %reduce-scatter.24.cloned.1.call-update) | async-done | bytes 147472 | tf_op jit(solution)/shard_map/reduce_scatter | solution.py:150
  520.0 48.1 %reduce-scatter.18.cloned.1.call-done = bf16[96,2304]{1,0:T(8,128)(2,1)} async-done(((bf16[768,2304]{1,0:T(8,128)(2,1)}), bf16[96,2304]{1,0:T(8,128)(2,1)}) %reduce-scatter.18.cloned.1.call-update) | async-done | bytes 442384 | tf_op jit(solution)/shard_map/reduce_scatter | solution.py:151
  574.1 39.5 %all-reduce.1 = f32[3072]{0:T(1024)S(1)} all-reduce(f32[3072]{0:T(1024)S(1)} %pad_maximum_fusion.4), channel_id=11, replica_groups=mesh['win'=4,'seq'=8] {'win','seq'}, use_global_device_ids=true, to_apply=%region_29.30.clone | all-reduce | flops 3072 | bytes 24576
  622.0 40.8 %psum.7 = f32[]{:T(128)} all-reduce(f32[]{:T(128)S(6)} %add.254), channel_id=1, replica_groups=mesh['win'=4,'seq'=8] {'win','seq'}, use_global_device_ids=true, to_apply=%region_31.32 | all-reduce | flops 1 | bytes 8 | tf_op jit(solution)/shard_map/psum | solution.py:163
  (197 shorter events, 123.5 us)
Async XLA Ops:
  7.2 37.1 %copy-start.27 = (f32[96]{0:T(128)S(1)}, f32[96]{0:T(128)}, u32[]{:S(2)}) copy-start(f32[96]{0:T(128)} %param.27) | copy-start | bytes 1156
  7.2 77.1 %copy-start.3 = (bf16[2,128,768]{2,1,0:T(8,128)(2,1)S(1)}, bf16[2,128,768]{2,1,0:T(8,128)(2,1)}, u32[]{:S(2)}) copy-start(bf16[2,128,768]{2,1,0:T(8,128)(2,1)} %param.19) | copy-start | bytes 1179652
  7.2 77.8 %all-gather.7.cloned.1.call-start = ((), (), s32[]{:S(2)}) async-start(), calls=%async_computation.9 | async-start | bytes 3981312 | tf_op jit(solution)/shard_map/all_gather | solution.py:78
  26.7 98.3 %all-gather.15.cloned.1.call-start = ((), (), s32[]{:S(2)}) async-start(), calls=%async_computation.13 | async-start | bytes 5308416 | tf_op jit(solution)/shard_map/all_gather | solution.py:78
  44.2 110.2 %all-gather.9.cloned.1.call-start = ((), (), s32[]{:S(2)}) async-start(), calls=%async_computation.10 | async-start | bytes 7077888 | tf_op jit(solution)/shard_map/all_gather | solution.py:92
  88.9 33.4 %copy-start.22 = (bf16[2,128,768]{2,1,0:T(8,128)(2,1)S(1)}, bf16[2,128,768]{2,1,0:T(8,128)(2,1)}, u32[]{:S(2)}) copy-start(bf16[2,128,768]{2,1,0:T(8,128)(2,1)} %param.20) | copy-start | bytes 1179652
  90.1 90.6 %all-gather.11.cloned.1.call-start = ((), (), s32[]{:S(2)}) async-start(), calls=%async_computation.11 | async-start | bytes 1327104 | tf_op jit(solution)/shard_map/all_gather | solution.py:78
  105.2 116.3 %all-gather.13.cloned.1.call-start = ((), (), s32[]{:S(2)}) async-start(), calls=%async_computation.12 | async-start | bytes 5308416 | tf_op jit(solution)/shard_map/all_gather | solution.py:78
  121.5 190.7 %reduce-scatter.20.cloned.1.call-start = ((), (), s32[]{:S(2)}) async-start(), calls=%async_computation.15 | async-start | bytes 1327104 | tf_op jit(solution)/shard_map/reduce_scatter | solution.py:151
  122.3 40.2 %copy-start.7 = (f32[2,2,12,1024]{3,1,2,0:T(2,128)}, f32[2,2,12,1024]{3,1,2,0:T(2,128)S(1)}, u32[]{:S(2)}) copy-start(f32[2,2,12,1024]{3,1,2,0:T(2,128)S(1)} %add.238) | copy-start | bytes 589828
  232.9 94.7 %reduce-scatter.26.cloned.1.call-start = ((), (), s32[]{:S(2)}) async-start(), calls=%async_computation.18 | async-start | bytes 5308416 | tf_op jit(solution)/shard_map/reduce_scatter | solution.py:151
  239.2 145.7 %reduce-scatter.22.cloned.1.call-start = ((), (), s32[]{:S(2)}) async-start(), calls=%async_computation.16 | async-start | bytes 5308416 | tf_op jit(solution)/shard_map/reduce_scatter | solution.py:151
  244.5 206.0 %reduce-scatter.28.cloned.1.call-start = ((), (), s32[]{:S(2)}) async-start(), calls=%async_computation.19 | async-start | bytes 7077888
  312.1 160.5 %reduce-scatter.32.cloned.1.call-start = ((), (), s32[]{:S(2)}) async-start(), calls=%async_computation.21 | async-start | bytes 245760
  313.9 181.2 %reduce-scatter.34.cloned.1.call-start = ((), (), s32[]{:S(2)}) async-start(), calls=%async_computation.22 | async-start | bytes 737280
  329.8 188.0 %reduce-scatter.24.cloned.1.call-start = ((), (), s32[]{:S(2)}) async-start(), calls=%async_computation.17 | async-start | bytes 737280 | tf_op jit(solution)/shard_map/reduce_scatter | solution.py:150
  385.0 183.2 %reduce-scatter.18.cloned.1.call-start = ((), (), s32[]{:S(2)}) async-start(), calls=%async_computation.14 | async-start | bytes 3981312 | tf_op jit(solution)/shard_map/reduce_scatter | solution.py:151
  392.1 62.9 %copy-start.10 = (bf16[256,768]{1,0:T(8,128)(2,1)S(1)}, bf16[256,768]{1,0:T(8,128)(2,1)}, u32[]{:S(2)}) copy-start(bf16[256,768]{1,0:T(8,128)(2,1)} %copy-done.9) | copy-start | bytes 1179652
  458.9 155.4 %reduce-scatter.30.cloned.1.call-start = ((), (), s32[]{:S(2)}) async-start(), calls=%async_computation.20 | async-start | bytes 737280
  573.6 90.0 %copy-start.11 = (f32[384,192]{1,0:T(8,128)S(1)}, f32[384,192]{1,0:T(8,128)}, u32[]{:S(2)}) copy-start(f32[384,192]{1,0:T(8,128)} %copy.171) | copy-start | bytes 884740
  573.6 90.0 %copy-start.12 = (f32[384,192]{1,0:T(8,128)S(1)}, f32[384,192]{1,0:T(8,128)}, u32[]{:S(2)}) copy-start(f32[384,192]{1,0:T(8,128)} %copy.172) | copy-start | bytes 884740
  622.0 45.5 %copy-start.28 = (f32[96]{0:T(128)S(1)}, f32[96]{0:T(128)}, u32[]{:S(2)}) copy-start(f32[96]{0:T(128)} %param.37) | copy-start | bytes 1156
  622.0 45.5 %copy-start.29 = (f32[96]{0:T(128)S(1)}, f32[96]{0:T(128)}, u32[]{:S(2)}) copy-start(f32[96]{0:T(128)} %param.32) | copy-start | bytes 1156
  622.0 46.1 %copy-start.21 = (f32[96,192]{1,0:T(8,128)S(1)}, f32[96,192]{1,0:T(8,128)}, u32[]{:S(2)}) copy-start(f32[96,192]{1,0:T(8,128)} %param.24) | copy-start | bytes 221188
  (24 other events, 198.2 us)
Sparse Core Ops, SparseCore 0:
  26.8 36.0 all-gather.6
  64.8 40.3 all-gather.14
  107.7 46.6 all-gather.8
  156.7 24.0 all-gather.10
  182.5 38.9 all-gather.12
  233.0 36.7 reduce-scatter.19
  273.7 53.8 reduce-scatter.25
  331.1 53.8 reduce-scatter.21
  388.7 61.7 reduce-scatter.27
  453.2 19.3 reduce-scatter.31
  474.9 20.1 reduce-scatter.33
  497.4 20.3 reduce-scatter.23
  521.6 46.4 reduce-scatter.17
  571.0 21.9 reduce-scatter.29
where the time goes:
time: 690 us; the launch traced here: 681 us
  waiting for transfers between devices  286 us (41%)
  blocking collectives  185 us (27%)
  matrix products  78.7 us (11%)
  local copies, waits for them, and re-layouts  69 us (10%)
  other arithmetic  41.1 us (6%)
  between operations  19.9 us (3%)
    reduce_scatter x4, waiting for transfers between devices, per_device(): lax.psum_scatter(raw.astype(jnp.bfloat16), 'seq', scatter_dimension=0, ti...  117 us
    unnamed x2, blocking collectives  79.3 us
    unnamed x18, waiting for transfers between devices  78.1 us
    all_gather x4, blocking collectives, per_device(): lax.all_gather(low, 'win', axis=1, tiled=True)  64.6 us
    unnamed x89, local copies, waits for them, and re-layouts  52.3 us
    all_gather x4, waiting for transfers between devices, per_device(): lax.all_gather(lax.all_gather(low, 'win', axis=1, tiled=True), 'seq', axi...  45.8 us
    psum x1, blocking collectives, per_device(): grad_norm = jnp.sqrt(lax.psum(local_squares, ('win', 'seq')))  40.8 us
    all_gather x1, waiting for transfers between devices, per_device(): window = lax.all_gather(keyval, 'seq', axis=1, tiled=True)  23.8 us
  transfers between devices with their start and end apart: 14, of which 10 were waited for; matrix products, arithmetic and copies ran while one was open for 23% of the time, Pallas kernels for 0%

commit v1 on v0

--- a/solution.py
+++ b/solution.py
@@ -89,7 +89,8 @@
     qkv = jnp.dot(h_one, full_qkv, preferred_element_type=jnp.float32)
     q_heads = qkv[:, :width].astype(jnp.bfloat16).reshape(wins, blocks_dev, BLK, H, HD)
     keyval = qkv[:, width:].astype(jnp.bfloat16).reshape(wins, local_len, 2 * width)
-    window = lax.all_gather(keyval, "seq", axis=1, tiled=True)
+    sent = jnp.stack([keyval] * lax.axis_size("seq"))
+    window = jnp.concatenate(lax.all_to_all(sent, "seq", 0, 0), axis=1)
     shaped = window.reshape(wins, block_count * BLK, 2, H, HD)
     keys, values = (shaped[:, :, 0], shaped[:, :, 1])
     scores = (

time: 690 us -> 706 us (1.023)
  local copies, waits for them, and re-layouts: 69 us -> 91.4 us
  waiting for transfers between devices: 286 us -> 275 us
    all_to_all x0 -> x1, waiting for transfers between devices: none -> 60.4 us  [per_device(): window = jnp.concatenate(lax.all_to_all(sent, 'seq', 0, 0), axis=1)]
    all_gather x4, waiting for transfers between devices: 45.8 us -> 0.08 us  [per_device(): lax.all_gather(lax.all_gather(low, 'win', axis=1, tiled=True), 'seq', axi...]
    all_gather x1 -> x0, waiting for transfers between devices: 23.8 us -> none  [per_device(): window = lax.all_gather(keyval, 'seq', axis=1, tiled=True)]
    another operation x0 -> x3, local copies, waits for them, and re-layouts: none -> 14.6 us  [the longest x1 10.3 us: per_device(): shaped = window.reshape(wins, block_count * BLK, 2, H, HD)]
    reshape x1, local copies, waits for them, and re-layouts: 1.15 us -> 8.67 us  [per_device(): window = jnp.concatenate(lax.all_to_all(sent, 'seq', 0, 0), axis=1)]
    unnamed x89 -> x91, local copies, waits for them, and re-layouts: 52.3 us -> 52.6 us
    unnamed x18 -> x17, waiting for transfers between devices: 78.1 us -> 78.1 us
  transfers between devices with their start and end apart: 14 -> 14, of which waited for: 10 -> 8; matrix products, arithmetic and copies ran while one was open for 23% -> 25% of each run, Pallas kernels for 0% -> 0%
where the time goes in v1:
time: 706 us; the launch traced here: 698 us
  waiting for transfers between devices  275 us (39%)
  blocking collectives  186 us (26%)
  local copies, waits for them, and re-layouts  91.4 us (13%)
  matrix products  79.2 us (11%)
  other arithmetic  40.6 us (6%)
  between operations  20 us (3%)
    reduce_scatter x4, waiting for transfers between devices, per_device(): lax.psum_scatter(raw.astype(jnp.bfloat16), 'seq', scatter_dimension=0, ti...  115 us
    unnamed x2, blocking collectives  79 us
    unnamed x17, waiting for transfers between devices  78.1 us
    all_gather x4, blocking collectives, per_device(): lax.all_gather(low, 'win', axis=1, tiled=True)  65.8 us
    all_to_all x1, waiting for transfers between devices, per_device(): window = jnp.concatenate(lax.all_to_all(sent, 'seq', 0, 0), axis=1)  60.4 us
    unnamed x91, local copies, waits for them, and re-layouts  52.6 us
    psum x1, blocking collectives, per_device(): grad_norm = jnp.sqrt(lax.psum(local_squares, ('win', 'seq')))  40.9 us
    reduce_scatter x1, waiting for transfers between devices, per_device(): lax.psum_scatter(lax.psum_scatter(raw.astype(jnp.bfloat16), 'seq', scatte...  21.6 us
  transfers between devices with their start and end apart: 14, of which 8 were waited for; matrix products, arithmetic and copies ran while one was open for 25% of the time, Pallas kernels for 0%

profile of v1, /device:TPU:0, one launch (start us, length us, event | category | flops | bytes accessed | tf_op | source)
XLA Modules:
  0.0 697.8 jit_solution(12916912149934830340)
XLA Ops:
  8.3 17.0 %all-gather = bf16[4,576,96]{1,2,0:T(8,128)(2,1)S(1)} all-gather(bf16[1,576,96]{1,2,0:T(8,128)(2,1)S(1)} %convert_bitcast_fusion), channel_id=1, replica_groups=mesh['win'=4,'seq'=8] {'win'}, dimensions={0}, use_global_device_ids=true | all-gather | bytes 552960 | tf_op jit(solution)/shard_map/all_gather | solution.py:78
  26.8 17.8 %all_gather.34 = bf16[384,768]{0,1:T(8,128)(2,1)} all-gather(bf16[384,192]{0,1:T(8,128)(2,1)S(1)} %convert_element_type.148), channel_id=1, replica_groups=mesh['win'=4,'seq'=8] {'win'}, dimensions={1}, use_global_device_ids=true | all-gather | bytes 737280 | tf_op jit(solution)/shard_map/all_gather | solution.py:78
  44.8 13.6 %all_gather.30 = bf16[96,768]{0,1:T(8,128)(2,1)S(1)} all-gather(bf16[96,192]{0,1:T(8,128)(2,1)S(1)} %copy.164), channel_id=1, replica_groups=mesh['win'=4,'seq'=8] {'win'}, dimensions={1}, use_global_device_ids=true | all-gather | bytes 184320 | tf_op jit(solution)/shard_map/all_gather | solution.py:78
  59.9 39.5 %all-reduce = bf16[3072]{0:T(1024)(128)(2,1)S(1)} all-reduce(bf16[3072]{0:T(1024)(128)(2,1)S(1)} %dynamic-update-slice), channel_id=1, replica_groups=mesh['win'=4,'seq'=8] {'win','seq'}, use_global_device_ids=true, to_apply=%add | all-reduce | flops 3072 | bytes 12288
  113.2 17.5 %all_gather.32 = bf16[96,3072]{1,0:T(8,128)(2,1)} all-gather(bf16[96,768]{1,0:T(8,128)(2,1)S(1)} %convert_element_type.146), channel_id=1, replica_groups=mesh['win'=4,'seq'=8] {'win'}, dimensions={1}, use_global_device_ids=true | all-gather | bytes 737280 | tf_op jit(solution)/shard_map/all_gather | solution.py:78
  138.9 60.4 %all-to-all-done = bf16[8,2,128,1536]{2,3,1,0:T(8,128)(2,1)} async-done(((bf16[8,2,128,1536]{2,3,1,0:T(8,128)(2,1)}), bf16[8,2,128,1536]{2,3,1,0:T(8,128)(2,1)}, u32[]{:S(2)}, u32[]{:S(2)}) %all-to-all-start) | async-done | bytes 6291488 | tf_op jit(solution)/shard_map/all_to_all | solution.py:93
  199.3 8.7 %copy.157 = bf16[2,8,128,1536]{2,1,3,0:T(8,128)(2,1)} copy(bf16[2,8,128,1536]{2,3,0,1:T(8,128)(2,1)} %bitcast.7) | data formatting | bytes 12582912 | tf_op jit(solution)/shard_map/reshape | solution.py:93
  208.0 10.3 %reshape_reshape.3 = bf16[2,1024,2,12,64]{1,4,3,2,0:T(8,128)(2,1)} reshape(bf16[2,8,128,1536]{2,1,3,0:T(8,128)(2,1)} %copy.157) | data formatting | bytes 12582912 | tf_op jit(solution)/shard_map/reshape;reshape | solution.py:94
  229.0 7.3 %fusion.30 = bf16[2,2,64,12,64]{2,4,1,3,0:T(8,128)(2,1)S(1)} fusion(bf16[2,2,12,64,1024]{4,3,1,2,0:T(8,128)(2,1)S(1)} %exponential_convert_fusion, bf16[2,1024,2,12,64]{1,4,3,2,0:T(8,128)(2,1)} %reshape_reshape.3), kind=kOutput, calls=%fused_computation.43 | convolution fusion | flops 402849792 | bytes 9830400 | tf_op jit(solution)/shard_map/wbhqk,wkhd->wbqhd/dot_general | solution.py:104
  239.7 8.0 %fusion.10 = (bf16[256,3072]{1,0:T(8,128)(2,1)S(1)}, f32[256,3072]{1,0:T(8,128)}) fusion(f32[256,3072]{1,0:T(8,128)} %fusion.66, bf16[768,3072]{1,0:T(8,128)(2,1)} %all-gather.10.cloned.1.call-done, f32[256,768]{1,0:T(8,128)S(1)} %get-tuple-element.196, f32[768]{0:T(1024)S(1)} %get-tuple-element.190, f32[768]{0:T(1024)S(1)} %get-tuple-element.189, ...), kind=kOutput, calls=%fused_computation.24 | convolution fusion | flops 1224671232 | bytes 13377536 | tf_op jit(solution)/shard_map/dot_general | solution.py:108
  251.5 6.3 convolution_convert_fusion
  280.7 7.8 %fusion = f32[2,2,12,64]{3,1,2,0:T(2,128)S(1)} fusion(f32[2,2,12,64,1024]{4,3,1,2,0:T(8,128)} %bitcast.169, bf16[2,2,12,64,1024]{4,3,1,2,0:T(8,128)(2,1)} %copy-done.1), kind=kLoop, calls=%fused_computation.2 | loop fusion | flops 9434112 | bytes 18886656 | tf_op jit(solution)/shard_map/reduce_sum | solution.py:129
  288.6 10.0 %fusion.1 = bf16[2,2,12,64,1024]{4,3,1,2,0:T(8,128)(2,1)S(1)} fusion(f32[2,2,12,64]{3,1,2,0:T(2,128)S(1)} %fusion, f32[2,12,1024,128]{2,3,1,0} %fusion.13, f32[2,2,12,64]{3,1,2,0:T(2,128)S(1)} %bitcast.188, f32[2,2,12,1024]{3,1,2,0:T(2,128)S(1)} %copy-done.8, f32[2,12,1024,128]{2,3,1,0} %copy-done), kind=kLoop, calls=%fused_computation.3 | loop fusion | flops 25165824 | bytes 31678464 | tf_op jit(solution)/shard_map/convert_element_type | solution.py:130
  307.6 16.6 %copy.187 = bf16[2,1024,1536]{2,0,1:T(2,128)(2,1)} copy(bf16[2,1024,1536]{1,2,0:T(8,128)(2,1)} %bitcast.171) | data formatting | bytes 12582912
  324.2 7.1 %copy.203 = bf16[128,8,2,1536]{3,1,2,0:T(8,128)(2,1)} copy(bf16[128,8,2,1536]{3,2,1,0:T(2,128)(2,1)} %bitcast.172) | data formatting | bytes 12582912
  333.2 11.4 %reduce-scatter.26.cloned.1.call-done = bf16[384,768]{1,0:T(8,128)(2,1)} async-done(((bf16[3072,768]{1,0:T(8,128)(2,1)}), bf16[384,768]{1,0:T(8,128)(2,1)}) %reduce-scatter.26.cloned.1.call-update) | async-done | bytes 589840 | tf_op jit(solution)/shard_map/reduce_scatter | solution.py:152
  346.9 55.2 %reduce-scatter.22.cloned.1.call-done = bf16[96,3072]{1,0:T(8,128)(2,1)} async-done(((bf16[768,3072]{1,0:T(8,128)(2,1)}), bf16[96,3072]{1,0:T(8,128)(2,1)}) %reduce-scatter.22.cloned.1.call-update) | async-done | bytes 589840 | tf_op jit(solution)/shard_map/reduce_scatter | solution.py:152
  402.3 6.9 fusion.33
  413.4 54.1 %reduce-scatter.28.cloned.1.call-done = bf16[128,3072]{1,0:T(8,128)(2,1)} async-done(((bf16[1024,3072]{1,0:T(8,128)(2,1)}), bf16[128,3072]{1,0:T(8,128)(2,1)}) %reduce-scatter.28.cloned.1.call-update) | async-done | bytes 786448
  491.3 20.9 %reduce-scatter.34.cloned.1.call-done = bf16[192,384]{1,0:T(8,128)(2,1)} async-done(((bf16[768,384]{1,0:T(8,128)(2,1)}), bf16[192,384]{1,0:T(8,128)(2,1)}) %reduce-scatter.34.cloned.1.call-update) | async-done | bytes 147472
  513.2 21.6 %reduce-scatter.24.cloned.1.call-done = bf16[96,768]{1,0:T(8,128)(2,1)} async-done(((bf16[96,3072]{1,0:T(8,128)(2,1)}), bf16[96,768]{1,0:T(8,128)(2,1)}) %reduce-scatter.24.cloned.1.call-update) | async-done | bytes 147472 | tf_op jit(solution)/shard_map/reduce_scatter | solution.py:151
  537.1 48.0 %reduce-scatter.18.cloned.1.call-done = bf16[96,2304]{1,0:T(8,128)(2,1)} async-done(((bf16[768,2304]{1,0:T(8,128)(2,1)}), bf16[96,2304]{1,0:T(8,128)(2,1)}) %reduce-scatter.18.cloned.1.call-update) | async-done | bytes 442384 | tf_op jit(solution)/shard_map/reduce_scatter | solution.py:152
  591.1 39.5 %all-reduce.1 = f32[3072]{0:T(1024)S(1)} all-reduce(f32[3072]{0:T(1024)S(1)} %pad_maximum_fusion.4), channel_id=11, replica_groups=mesh['win'=4,'seq'=8] {'win','seq'}, use_global_device_ids=true, to_apply=%region_29.30.clone | all-reduce | flops 3072 | bytes 24576
  639.0 40.9 %psum.7 = f32[]{:T(128)} all-reduce(f32[]{:T(128)S(6)} %add.254), channel_id=1, replica_groups=mesh['win'=4,'seq'=8] {'win','seq'}, use_global_device_ids=true, to_apply=%region_31.32 | all-reduce | flops 1 | bytes 8 | tf_op jit(solution)/shard_map/psum | solution.py:164
  (202 shorter events, 131.5 us)
Async XLA Ops:
  7.2 37.5 %copy-start.21 = (f32[96,192]{1,0:T(8,128)S(1)}, f32[96,192]{1,0:T(8,128)}, u32[]{:S(2)}) copy-start(f32[96,192]{1,0:T(8,128)} %param.24) | copy-start | bytes 221188
  7.2 52.0 %copy-start.28 = (f32[96]{0:T(128)S(1)}, f32[96]{0:T(128)}, u32[]{:S(2)}) copy-start(f32[96]{0:T(128)} %param.27) | copy-start | bytes 1156
  7.2 52.0 %copy-start.3 = (bf16[2,128,768]{2,1,0:T(8,128)(2,1)S(1)}, bf16[2,128,768]{2,1,0:T(8,128)(2,1)}, u32[]{:S(2)}) copy-start(bf16[2,128,768]{2,1,0:T(8,128)(2,1)} %param.19) | copy-start | bytes 1179652
  7.2 92.4 %all-gather.6.cloned.1.call-start = ((), (), s32[]{:S(2)}) async-start(), calls=%async_computation.10 | async-start | bytes 3981312 | tf_op jit(solution)/shard_map/all_gather | solution.py:78
  26.8 106.8 %all-gather.12.cloned.1.call-start = ((), (), s32[]{:S(2)}) async-start(), calls=%async_computation.13 | async-start | bytes 5308416 | tf_op jit(solution)/shard_map/all_gather | solution.py:78
  44.6 193.0 %all-gather.8.cloned.1.call-start = ((), (), s32[]{:S(2)}) async-start(), calls=%async_computation.11 | async-start | bytes 1327104 | tf_op jit(solution)/shard_map/all_gather | solution.py:78
  108.2 91.1 %all-to-all-start = ((bf16[8,2,128,1536]{2,3,1,0:T(8,128)(2,1)}), bf16[8,2,128,1536]{2,3,1,0:T(8,128)(2,1)}, u32[]{:S(2)}, u32[]{:S(2)}) async-start(bf16[8,2,128,1536]{2,3,1,0:T(8,128)(2,1)} %stack.15), calls=%async_computation | async-start | bytes 12582912 | tf_op jit(solution)/shard_map/all_to_all | solution.py:93
  113.1 126.6 %all-gather.10.cloned.1.call-start = ((), (), s32[]{:S(2)}) async-start(), calls=%async_computation.12 | async-start | bytes 5308416 | tf_op jit(solution)/shard_map/all_gather | solution.py:78
  130.7 200.7 %reduce-scatter.20.cloned.1.call-start = ((), (), s32[]{:S(2)}) async-start(), calls=%async_computation.15 | async-start | bytes 1327104 | tf_op jit(solution)/shard_map/reduce_scatter | solution.py:152
  131.6 94.7 %copy-start.7 = (f32[2,2,12,1024]{3,1,2,0:T(2,128)}, f32[2,2,12,1024]{3,1,2,0:T(2,128)S(1)}, u32[]{:S(2)}) copy-start(f32[2,2,12,1024]{3,1,2,0:T(2,128)S(1)} %add.238) | copy-start | bytes 589828
  251.4 93.2 %reduce-scatter.26.cloned.1.call-start = ((), (), s32[]{:S(2)}) async-start(), calls=%async_computation.18 | async-start | bytes 5308416 | tf_op jit(solution)/shard_map/reduce_scatter | solution.py:152
  257.8 144.3 %reduce-scatter.22.cloned.1.call-start = ((), (), s32[]{:S(2)}) async-start(), calls=%async_computation.16 | async-start | bytes 5308416 | tf_op jit(solution)/shard_map/reduce_scatter | solution.py:152
  263.1 204.5 %reduce-scatter.28.cloned.1.call-start = ((), (), s32[]{:S(2)}) async-start(), calls=%async_computation.19 | async-start | bytes 7077888
  331.3 158.4 %reduce-scatter.32.cloned.1.call-start = ((), (), s32[]{:S(2)}) async-start(), calls=%async_computation.21 | async-start | bytes 245760
  333.2 179.0 %reduce-scatter.34.cloned.1.call-start = ((), (), s32[]{:S(2)}) async-start(), calls=%async_computation.22 | async-start | bytes 737280
  346.8 188.0 %reduce-scatter.24.cloned.1.call-start = ((), (), s32[]{:S(2)}) async-start(), calls=%async_computation.17 | async-start | bytes 737280 | tf_op jit(solution)/shard_map/reduce_scatter | solution.py:151
  402.1 183.1 %reduce-scatter.18.cloned.1.call-start = ((), (), s32[]{:S(2)}) async-start(), calls=%async_computation.14 | async-start | bytes 3981312 | tf_op jit(solution)/shard_map/reduce_scatter | solution.py:152
  409.1 62.9 %copy-start.10 = (bf16[256,768]{1,0:T(8,128)(2,1)S(1)}, bf16[256,768]{1,0:T(8,128)(2,1)}, u32[]{:S(2)}) copy-start(bf16[256,768]{1,0:T(8,128)(2,1)} %copy-done.9) | copy-start | bytes 1179652
  475.9 155.4 %reduce-scatter.30.cloned.1.call-start = ((), (), s32[]{:S(2)}) async-start(), calls=%async_computation.20 | async-start | bytes 737280
  590.6 90.0 %copy-start.11 = (f32[384,192]{1,0:T(8,128)S(1)}, f32[384,192]{1,0:T(8,128)}, u32[]{:S(2)}) copy-start(f32[384,192]{1,0:T(8,128)} %copy.174) | copy-start | bytes 884740
  590.6 90.0 %copy-start.12 = (f32[384,192]{1,0:T(8,128)S(1)}, f32[384,192]{1,0:T(8,128)}, u32[]{:S(2)}) copy-start(f32[384,192]{1,0:T(8,128)} %copy.175) | copy-start | bytes 884740
  639.0 45.5 %copy-start.29 = (f32[96]{0:T(128)S(1)}, f32[96]{0:T(128)}, u32[]{:S(2)}) copy-start(f32[96]{0:T(128)} %param.37) | copy-start | bytes 1156
  639.0 45.5 %copy-start.30 = (f32[96]{0:T(128)S(1)}, f32[96]{0:T(128)}, u32[]{:S(2)}) copy-start(f32[96]{0:T(128)} %param.32) | copy-start | bytes 1156
  639.0 46.1 %copy-start.22 = (f32[96,192]{1,0:T(8,128)S(1)}, f32[96,192]{1,0:T(8,128)}, u32[]{:S(2)}) copy-start(f32[96,192]{1,0:T(8,128)} %param.24) | copy-start | bytes 221188
  (26 other events, 213.2 us)
Sparse Core Ops, SparseCore 0:
  26.9 35.7 all-gather.5
  64.5 40.3 all-gather.11
  107.4 53.0 all-gather.7
  162.2 47.7 all-gather.9
  251.5 35.4 reduce-scatter.19
  290.7 53.8 reduce-scatter.25
  348.1 53.8 reduce-scatter.21
  405.8 61.7 reduce-scatter.27
  470.4 19.3 reduce-scatter.31
  492.0 20.1 reduce-scatter.33
  514.6 20.2 reduce-scatter.23
  538.6 46.5 reduce-scatter.17
  588.1 21.8 reduce-scatter.29
